TPU v7x, 256 devices: a whole 4x4x8 slice. The times are simulated.
256 devices in a mesh: leaf: 16 (over y, x), sep: 8 (over z), mode: 2 (over core).
Axes of the slice: x: 4, y: 4, z: 8, core: 2. Of those that a mesh axis runs over, the one named last changes fastest.
Arguments:
- modes: bfloat16 [1024, 2048, 256], P(('leaf', 'sep'), 'mode'), may hold values from -0.125 to 0.125
- coupling: bfloat16 [1024, 2048, 256], P(('leaf', 'sep'), 'mode'), may hold values from -6 to 6
- eigenvalues: float32 [1024, 256], P(('leaf', 'sep'), 'mode'), may hold values from 200 to 4000
- separator_of: int32 [1024, 1], P(('leaf', 'sep')), may hold values from 0 to 7; in each aligned block of 8 rows (0 to 7, 8 to 15, ...) at most 2 rows name the same one
- row_offset: int32 [1024], P(('leaf', 'sep')), may hold values from 0 to 256
- stiffness: bfloat16 [8, 512, 512], P('sep', None, ('leaf', 'mode')), may hold values from -1 to 40
- start_block: bfloat16 [8, 512, 256], P('sep', ('leaf', 'mode')), may hold values from -40 to 40
- rotations: bfloat16 [8, 2, 256, 256], P('sep'), may hold values from -0.375 to 0.375
Outputs:
- subspace: bfloat16 [8, 512, 256], P('sep', ('leaf', 'mode'))
- column_norms: float32 [8, 2, 256], P('sep')
Inputs may be any that keep to these rules, and one draw needn't show every extreme that they name: `separator_of`: among the 8 leaves of one device at most 2 couple to one separator, and in every draw some separator gets exactly 2 of them.
All inputs are finite; a program needn't handle non-finite values.
Results may differ from a plain program's by a relative error of at most 0.0075.
Values may be sent and summed in bfloat16 or wider, within the bound.
No kernel may reach another device: no remote copies, remote signals or barrier semaphores. Data moves between devices by JAX's collectives and lax.ppermute only.
A program may use at most 64 MiB of HBM per device.

v0:
```python
import jax
import jax.numpy as jnp
from jax import lax
from jax.sharding import PartitionSpec as P

SEP_ROWS = 512
CAP = 2
ITERS = 2
epsilon = 1e-06


def leaf_projection(modes, coupling, eigenvalues):
    summed = lax.psum_scatter(
        jnp.einsum("ldm,ldw->mlw", modes, coupling, preferred_element_type=jnp.float32),
        "mode",
        scatter_dimension=0,
        tiled=True,
    )
    return (summed / jnp.sqrt(eigenvalues.T)[:, :, None]).astype(jnp.bfloat16)


def route_blocks(scaled, separator_of, row_offset):
    groups = lax.axis_size("sep")
    leaves = scaled.shape[1]
    target = separator_of[:, 0]
    leaf_order = jnp.arange(leaves)
    earlier = (target[:, None] == target[None, :]) & (leaf_order[None, :] < leaf_order[:, None])
    position = jnp.sum(earlier.astype(jnp.int32), 1)
    slot_of = target * CAP + position
    slot_table = slot_of[None, :] == jnp.arange(groups * CAP)[:, None]
    send_blocks = jnp.einsum(
        "sl,mlw->smw", slot_table.astype(jnp.bfloat16), scaled, preferred_element_type=jnp.float32
    ).astype(jnp.bfloat16)
    send_offsets = jnp.sum(jnp.where(slot_table, row_offset[None, :], 0), 1)
    block_shape = (groups, CAP, send_blocks.shape[1], send_blocks.shape[2])
    got_blocks, got_offsets = (
        lax.all_to_all(
            send_blocks.reshape(block_shape), "sep", split_axis=0, concat_axis=0, tiled=True
        ),
        lax.all_to_all(
            send_offsets.reshape(groups, CAP), "sep", split_axis=0, concat_axis=0, tiled=True
        ),
    )
    return (
        got_blocks.reshape(groups * CAP, block_shape[2], block_shape[3]),
        got_offsets.reshape(groups * CAP),
    )


def coupled_correction(full_block, blocks, offsets):
    width_rows = blocks.shape[2]

    def add_slot(slot_index, accumulated):
        offset = offsets[slot_index]
        weights = blocks[slot_index]
        window = lax.dynamic_slice_in_dim(full_block, offset, width_rows, 0)
        projected = jnp.dot(weights, window, preferred_element_type=jnp.float32).astype(
            jnp.bfloat16
        )
        update = jnp.einsum("mw,mc->wc", weights, projected, preferred_element_type=jnp.float32)
        current = lax.dynamic_slice_in_dim(accumulated, offset, width_rows, 0)
        return lax.dynamic_update_slice_in_dim(accumulated, current + update, offset, 0)

    initial = jnp.zeros(full_block.shape, jnp.float32)
    return lax.fori_loop(0, blocks.shape[0], add_slot, initial)


def gather_rows(own_block):
    return lax.all_gather(own_block, ("leaf", "mode"), axis=0, tiled=True)


def per_device(
    modes, coupling, eigenvalues, separator_of, row_offset, stiffness, start_block, rotations
):
    scaled = leaf_projection(modes, coupling, eigenvalues)
    blocks, offsets = route_blocks(scaled, separator_of, row_offset)
    stiff_columns = stiffness[0]
    own_block = start_block[0]
    ritz_turns = rotations[0]
    own_rows = own_block.shape[0]
    norm_list = []
    for iteration in range(ITERS):
        full_block = gather_rows(own_block)
        correction = coupled_correction(full_block, blocks, offsets)

        def assemble_rows(first_row, row_count, block_now=own_block, correction_now=correction):
            product = jnp.dot(stiff_columns, block_now, preferred_element_type=jnp.float32)
            return product - correction_now

        summed = lax.psum_scatter(
            assemble_rows(jnp.int32(0), lax.axis_size(("leaf", "mode")) * own_rows),
            ("leaf", "mode"),
            scatter_dimension=0,
            tiled=True,
        )
        squares = lax.psum(jnp.sum(summed * summed, 0), ("leaf", "mode"))
        column_scale = jnp.sqrt(squares / SEP_ROWS + epsilon)
        normed = (summed / column_scale).astype(jnp.bfloat16)
        own_block = jnp.dot(
            normed, ritz_turns[iteration], preferred_element_type=jnp.float32
        ).astype(jnp.bfloat16)
        norm_list.append(column_scale)
    return (own_block[None], jnp.stack(norm_list)[None])


def solution(mesh):
    in_specs = (
        P(("leaf", "sep"), "mode", None),
        P(("leaf", "sep"), "mode", None),
        P(("leaf", "sep"), "mode"),
        P(("leaf", "sep"), None),
        P(("leaf", "sep")),
        P("sep", None, ("leaf", "mode")),
        P("sep", ("leaf", "mode"), None),
        P("sep", None, None, None),
    )
    out_specs = (P("sep", ("leaf", "mode"), None), P("sep", None, None))
    return jax.shard_map(
        per_device, mesh=mesh, in_specs=in_specs, out_specs=out_specs, check_vma=False
    )
```

profile of v0, /device:TPU:1, one launch (start us, length us, event | category | flops | bytes accessed | tf_op | source)
XLA Modules:
  0.0 560.8 jit_solution(13401757239637969915)
XLA Ops:
  7.3 6.2 %convolution_bitcast_fusion = f32[256,8,256]{0,2,1:T(8,128)} fusion(bf16[8,1024,256]{2,1,0:T(8,128)(2,1)} %param.13, bf16[8,1024,256]{2,1,0:T(8,128)(2,1)} %param.12), kind=kOutput, calls=%fused_computation.13 | convolution fusion | flops 1073741824 | bytes 10485760 | tf_op jit(solution)/shard_map/ldm,ldw->mlw/dot_general | solution.py:14
  14.5 9.0 %all-to-all-start = ((s32[8,1,2]{2,1,0:T(1,128)}), s32[8,1,2]{2,1,0:T(1,128)S(1)}, u32[]{:S(2)}, u32[]{:S(2)}) async-start(s32[8,1,2]{2,1,0:T(1,128)} %bitcast.7), calls=%async_computation | async-start | bytes 8192 | tf_op jit(solution)/shard_map/all_to_all | solution.py:40
  23.5 9.3 %reduce-scatter.6.cloned.1.call-done = f32[128,8,256]{0,2,1:T(8,128)} async-done(((f32[256,8,256]{0,2,1:T(8,128)}), f32[128,8,256]{0,2,1:T(8,128)}) %reduce-scatter.6.cloned.1.call-update) | async-done | bytes 1048592 | tf_op jit(solution)/shard_map/reduce_scatter | solution.py:13
  37.3 6.8 %all-to-all-start.1 = ((bf16[8,2,128,256]{3,1,2,0:T(2,128)(2,1)}), bf16[8,2,128,256]{3,1,2,0:T(2,128)(2,1)S(1)}, u32[]{:S(2)}, u32[]{:S(2)}) async-start(bf16[8,2,128,256]{3,1,2,0:T(2,128)(2,1)} %copy.30), calls=%async_computation.2 | async-start | bytes 2097152 | tf_op jit(solution)/shard_map/all_to_all | solution.py:37
  44.2 25.3 %all-gather = bf16[1,512,256]{2,1,0:T(8,128)(2,1)S(1)} all-gather(bf16[1,16,256]{2,1,0:T(8,128)(2,1)S(1)} %copy-done.1), channel_id=2, replica_groups=mesh['leaf'=16,'sep'=8,'mode'=2] {'leaf','mode'}, dimensions={1}, use_global_device_ids=true | all-gather | bytes 270336 | tf_op jit(solution)/shard_map/all_gather | solution.py:69
  70.8 2.6 all-to-all-done.1
  73.6 74.0 %while.26 = (s32[]{:T(128)}, f32[512,256]{1,0:T(8,128)S(1)}, s32[16]{0:T(128)S(1)}, bf16[16,128,256]{2,1,0:T(8,128)(2,1)S(1)}, bf16[512,256]{1,0:T(8,128)(2,1)S(1)}, /*index=5*/s32[]{:T(128)}, s32[]{:T(128)}, s32[]{:T(128)}) while((s32[]{:T(128)}, f32[512,256]{1,0:T(8,128)S(1)}, s32[16]{0:T(128)S(1)}, bf16[16,128,256]{2,1,0:T(8,128)(2,1)S(1)}, ...), condition=%wide.region_4.5_spmd, body=%wide.region_3.4_spmd.sunk | while | flops 33652740 | bytes 1312903 | solution.py:65
  148.8 80.6 %reduce-scatter.8.cloned.1.call-done = f32[16,256]{1,0:T(8,128)} async-done(((f32[512,256]{1,0:T(8,128)}), f32[16,256]{1,0:T(8,128)}) %reduce-scatter.8.cloned.1.call-update) | async-done | bytes 16400 | tf_op jit(solution)/shard_map/reduce_scatter | solution.py:90
  230.1 64.6 %psum.14 = f32[256]{0:T(256)S(1)} all-reduce(f32[256]{0:T(256)S(1)} %multiply_reduce_fusion.1), channel_id=1, replica_groups=mesh['leaf'=16,'sep'=8,'mode'=2] {'leaf','mode'}, use_global_device_ids=true, to_apply=%region_7.8 | all-reduce | flops 256 | bytes 2048 | tf_op jit(solution)/shard_map/psum | solution.py:96
  295.6 22.6 %all_gather.7 = bf16[512,256]{1,0:T(8,128)(2,1)S(1)} all-gather(bf16[16,256]{1,0:T(8,128)(2,1)S(1)} %convolution_convert_fusion.4), channel_id=1, replica_groups=mesh['leaf'=16,'sep'=8,'mode'=2] {'leaf','mode'}, dimensions={0}, use_global_device_ids=true | all-gather | bytes 270336 | tf_op jit(solution)/shard_map/all_gather | solution.py:69
  318.3 85.1 %while.27 = (s32[]{:T(128)}, f32[512,256]{0,1:T(8,128)S(1)}, s32[16]{0:T(128)S(1)}, bf16[16,128,256]{2,1,0:T(8,128)(2,1)S(1)}, bf16[512,256]{1,0:T(8,128)(2,1)S(1)}, /*index=5*/s32[]{:T(128)}, s32[]{:T(128)}, s32[]{:T(128)}) while((s32[]{:T(128)}, f32[512,256]{0,1:T(8,128)S(1)}, s32[16]{0:T(128)S(1)}, bf16[16,128,256]{2,1,0:T(8,128)(2,1)S(1)}, ...), condition=%wide.region_9.10_spmd, body=%wide.region_8.9_spmd.sunk | while | flops 33652740 | bytes 2884751 | solution.py:65
  326.8 1.9 dynamic_update_slice.17
  332.1 1.9 dynamic_update_slice.17
  337.4 1.9 dynamic_update_slice.17
  347.9 1.9 dynamic_update_slice.17
  353.1 2.2 dynamic_update_slice.17
  358.7 1.9 dynamic_update_slice.17
  369.2 1.9 dynamic_update_slice.17
  374.5 2.2 dynamic_update_slice.17
  390.6 1.9 dynamic_update_slice.17
  395.8 2.2 dynamic_update_slice.17
  401.4 1.9 dynamic_update_slice.17
  404.7 82.7 %reduce-scatter.10.cloned.1.call-done = f32[16,256]{1,0:T(8,128)} async-done(((f32[512,256]{1,0:T(8,128)}), f32[16,256]{1,0:T(8,128)}) %reduce-scatter.10.cloned.1.call-update) | async-done | bytes 16400
  488.2 64.6 %psum.15 = f32[256]{0:T(256)S(1)} all-reduce(f32[256]{0:T(256)S(1)} %multiply_reduce_fusion), channel_id=1, replica_groups=mesh['leaf'=16,'sep'=8,'mode'=2] {'leaf','mode'}, use_global_device_ids=true, to_apply=%region_12.13 | all-reduce | flops 256 | bytes 2048 | tf_op jit(solution)/shard_map/psum | solution.py:96
  (179 shorter events, 86.9 us)
Async XLA Ops:
  7.2 140.5 %copy-start = (bf16[1,512,16]{1,2,0:T(8,128)(2,1)S(1)}, bf16[1,512,16]{1,2,0:T(8,128)(2,1)}, u32[]{:S(2)}) copy-start(bf16[1,512,16]{1,2,0:T(8,128)(2,1)} %param.17) | copy-start | bytes 49156
  7.2 6.3 %copy-start.4 = (s32[8,1]{0,1:T(1,128)S(1)}, s32[8,1]{0,1:T(1,128)}, u32[]{:S(2)}) copy-start(s32[8,1]{0,1:T(1,128)} %param.15) | copy-start | bytes 100
  7.2 6.5 %copy-start.5 = (s32[8]{0:T(128)S(1)}, s32[8]{0:T(128)}, u32[]{:S(2)}) copy-start(s32[8]{0:T(128)} %param.16) | copy-start | bytes 100
  7.2 16.3 %copy-start.2 = (f32[8,128]{1,0:T(8,128)S(1)}, f32[8,128]{1,0:T(8,128)}, u32[]{:S(2)}) copy-start(f32[8,128]{1,0:T(8,128)} %param.14) | copy-start | bytes 12292
  7.2 25.6 %reduce-scatter.6.cloned.1.call-start = ((), (), s32[]{:S(2)}) async-start(), calls=%async_computation.5 | async-start | bytes 3145728 | tf_op jit(solution)/shard_map/reduce_scatter | solution.py:13
  14.5 22.9 %all-to-all-start = ((s32[8,1,2]{2,1,0:T(1,128)}), s32[8,1,2]{2,1,0:T(1,128)S(1)}, u32[]{:S(2)}, u32[]{:S(2)}) async-start(s32[8,1,2]{2,1,0:T(1,128)} %bitcast.7), calls=%async_computation | async-start | bytes 8192 | tf_op jit(solution)/shard_map/all_to_all | solution.py:40
  34.5 9.6 %copy-start.1 = (bf16[1,16,256]{2,1,0:T(8,128)(2,1)S(1)}, bf16[1,16,256]{2,1,0:T(8,128)(2,1)}, u32[]{:S(2)}) copy-start(bf16[1,16,256]{2,1,0:T(8,128)(2,1)} %param.18) | copy-start | bytes 24580
  37.3 36.0 %all-to-all-start.1 = ((bf16[8,2,128,256]{3,1,2,0:T(2,128)(2,1)}), bf16[8,2,128,256]{3,1,2,0:T(2,128)(2,1)S(1)}, u32[]{:S(2)}, u32[]{:S(2)}) async-start(bf16[8,2,128,256]{3,1,2,0:T(2,128)(2,1)} %copy.30), calls=%async_computation.2 | async-start | bytes 2097152 | tf_op jit(solution)/shard_map/all_to_all | solution.py:37
  44.1 185.3 %reduce-scatter.8.cloned.1.call-start = ((), (), s32[]{:S(2)}) async-start(), calls=%async_computation.6 | async-start | bytes 540672 | tf_op jit(solution)/shard_map/reduce_scatter | solution.py:90
  73.6 221.1 %copy-start.3 = (bf16[1,2,256,256]{3,2,1,0:T(8,128)(2,1)S(1)}, bf16[1,2,256,256]{3,2,1,0:T(8,128)(2,1)}, u32[]{:S(2)}) copy-start(bf16[1,2,256,256]{3,2,1,0:T(8,128)(2,1)} %param.19) | copy-start | bytes 786436
  148.7 338.6 %reduce-scatter.10.cloned.1.call-start = ((), (), s32[]{:S(2)}) async-start(), calls=%async_computation.7 | async-start | bytes 540672
Sparse Core Ops, SparseCore 0:
  13.6 19.1 reduce-scatter.5
  148.9 80.5 reduce-scatter.7
  404.8 82.4 reduce-scatter.9
where the time goes:
time: 562 us; the launch traced here: 561 us
  blocking collectives  177 us (31%)
  waiting for transfers between devices  175 us (31%)
  local copies, waits for them, and re-layouts  89.7 us (16%)
  loops' own time  63.5 us (11%)
  matrix products  21.7 us (4%)
  starting transfers between devices  15.9 us (3%)
  between operations  13.9 us (2%)
    psum x2, blocking collectives, per_device(): squares = lax.psum(jnp.sum(summed * summed, 0), ('leaf', 'mode'))  129 us
    unnamed x4, waiting for transfers between devices  82.7 us
    reduce_scatter x1, waiting for transfers between devices, per_device(): lax.psum_scatter(assemble_rows(jnp.int32(0), lax.axis_size(('leaf', 'mode...  80.6 us
    another operation x2, loops' own time, coupled_correction(): return lax.fori_loop(0, blocks.shape[0], add_slot, initial)  63.5 us
    dynamic_update_slice x48, local copies, waits for them, and re-layouts, add_slot(): lax.dynamic_update_slice_in_dim(accumulated, current + update, offset, 0)  60.6 us
    all_gather x2, blocking collectives, gather_rows(): return lax.all_gather(own_block, ('leaf', 'mode'), axis=0, tiled=True)  48 us
    dynamic_slice x32, local copies, waits for them, and re-layouts, add_slot(): offset = offsets[slot_index]  18.8 us
    dot_general x32, matrix products, add_slot(): jnp.einsum('mw,mc->wc', weights, projected, preferred_element_type=jnp.fl...  11.9 us
  transfers between devices with their start and end apart: 5, of which 4 were waited for; matrix products, arithmetic and copies ran while one was open for 1% of the time, Pallas kernels for 0%

commit v1 on v0

--- a/solution.py
+++ b/solution.py
@@ -93,7 +93,7 @@
             scatter_dimension=0,
             tiled=True,
         )
-        squares = lax.psum(jnp.sum(summed * summed, 0), ("leaf", "mode"))
+        squares = lax.psum(lax.psum(jnp.sum(summed * summed, 0), "mode"), "leaf")
         column_scale = jnp.sqrt(squares / SEP_ROWS + epsilon)
         normed = (summed / column_scale).astype(jnp.bfloat16)
         own_block = jnp.dot(

time: 562 us -> 517 us (0.920); the launches traced: 561 us -> 509 us
  blocking collectives: 177 us -> 126 us
    psum x2 -> x4, blocking collectives: 129 us -> 70.8 us  [per_device(): squares = lax.psum(lax.psum(jnp.sum(summed * summed, 0), 'mode'), 'leaf')]
    all_gather x2, blocking collectives: 48 us -> 54.7 us  [gather_rows(): return lax.all_gather(own_block, ('leaf', 'mode'), axis=0, tiled=True)]
where the time goes in v1:
time: 517 us; the launch traced here: 509 us
  waiting for transfers between devices  175 us (34%)
  blocking collectives  126 us (24%)
  local copies, waits for them, and re-layouts  89.7 us (17%)
  loops' own time  63.5 us (12%)
  matrix products  21.7 us (4%)
  starting transfers between devices  15.9 us (3%)
  between operations  13.9 us (3%)
    unnamed x4, waiting for transfers between devices  82.9 us
    reduce_scatter x1, waiting for transfers between devices, per_device(): lax.psum_scatter(assemble_rows(jnp.int32(0), lax.axis_size(('leaf', 'mode...  80.6 us
    psum x4, blocking collectives, per_device(): squares = lax.psum(lax.psum(jnp.sum(summed * summed, 0), 'mode'), 'leaf')  70.8 us
    another operation x2, loops' own time, coupled_correction(): return lax.fori_loop(0, blocks.shape[0], add_slot, initial)  63.5 us
    dynamic_update_slice x48, local copies, waits for them, and re-layouts, add_slot(): lax.dynamic_update_slice_in_dim(accumulated, current + update, offset, 0)  60.6 us
    all_gather x2, blocking collectives, gather_rows(): return lax.all_gather(own_block, ('leaf', 'mode'), axis=0, tiled=True)  54.7 us
    dynamic_slice x32, local copies, waits for them, and re-layouts, add_slot(): offset = offsets[slot_index]  18.8 us
    dot_general x32, matrix products, add_slot(): jnp.einsum('mw,mc->wc', weights, projected, preferred_element_type=jnp.fl...  11.9 us
  transfers between devices with their start and end apart: 5, of which 4 were waited for; matrix products, arithmetic and copies ran while one was open for 1% of the time, Pallas kernels for 0%

profile of v1, /device:TPU:1, one launch (start us, length us, event | category | flops | bytes accessed | tf_op | source)
XLA Modules:
  0.0 509.4 jit_solution(4798464849297094999)
XLA Ops:
  7.3 6.2 %convolution_bitcast_fusion = f32[256,8,256]{0,2,1:T(8,128)} fusion(bf16[8,1024,256]{2,1,0:T(8,128)(2,1)} %param.13, bf16[8,1024,256]{2,1,0:T(8,128)(2,1)} %param.12), kind=kOutput, calls=%fused_computation.13 | convolution fusion | flops 1073741824 | bytes 10485760 | tf_op jit(solution)/shard_map/ldm,ldw->mlw/dot_general | solution.py:14
  14.5 9.0 %all-to-all-start = ((s32[8,1,2]{2,1,0:T(1,128)}), s32[8,1,2]{2,1,0:T(1,128)S(1)}, u32[]{:S(2)}, u32[]{:S(2)}) async-start(s32[8,1,2]{2,1,0:T(1,128)} %bitcast.7), calls=%async_computation | async-start | bytes 8192 | tf_op jit(solution)/shard_map/all_to_all | solution.py:40
  23.5 9.3 %reduce-scatter.6.cloned.1.call-done = f32[128,8,256]{0,2,1:T(8,128)} async-done(((f32[256,8,256]{0,2,1:T(8,128)}), f32[128,8,256]{0,2,1:T(8,128)}) %reduce-scatter.6.cloned.1.call-update) | async-done | bytes 1048592 | tf_op jit(solution)/shard_map/reduce_scatter | solution.py:13
  37.3 6.8 %all-to-all-start.1 = ((bf16[8,2,128,256]{3,1,2,0:T(2,128)(2,1)}), bf16[8,2,128,256]{3,1,2,0:T(2,128)(2,1)S(1)}, u32[]{:S(2)}, u32[]{:S(2)}) async-start(bf16[8,2,128,256]{3,1,2,0:T(2,128)(2,1)} %copy.30), calls=%async_computation.2 | async-start | bytes 2097152 | tf_op jit(solution)/shard_map/all_to_all | solution.py:37
  44.2 25.3 %all-gather = bf16[1,512,256]{2,1,0:T(8,128)(2,1)S(1)} all-gather(bf16[1,16,256]{2,1,0:T(8,128)(2,1)S(1)} %copy-done.1), channel_id=2, replica_groups=mesh['leaf'=16,'sep'=8,'mode'=2] {'leaf','mode'}, dimensions={1}, use_global_device_ids=true | all-gather | bytes 270336 | tf_op jit(solution)/shard_map/all_gather | solution.py:69
  70.8 2.6 all-to-all-done.1
  73.6 74.0 %while.26 = (s32[]{:T(128)}, f32[512,256]{1,0:T(8,128)S(1)}, s32[16]{0:T(128)S(1)}, bf16[16,128,256]{2,1,0:T(8,128)(2,1)S(1)}, bf16[512,256]{1,0:T(8,128)(2,1)S(1)}, /*index=5*/s32[]{:T(128)}, s32[]{:T(128)}, s32[]{:T(128)}) while((s32[]{:T(128)}, f32[512,256]{1,0:T(8,128)S(1)}, s32[16]{0:T(128)S(1)}, bf16[16,128,256]{2,1,0:T(8,128)(2,1)S(1)}, ...), condition=%wide.region_4.5_spmd, body=%wide.region_3.4_spmd.sunk | while | flops 33652740 | bytes 1312903 | solution.py:65
  148.8 80.6 %reduce-scatter.8.cloned.1.call-done = f32[16,256]{1,0:T(8,128)} async-done(((f32[512,256]{1,0:T(8,128)}), f32[16,256]{1,0:T(8,128)}) %reduce-scatter.8.cloned.1.call-update) | async-done | bytes 16400 | tf_op jit(solution)/shard_map/reduce_scatter | solution.py:90
  230.1 4.7 psum.28
  234.8 30.8 %psum.29 = f32[256]{0:T(256)S(1)} all-reduce(f32[256]{0:T(256)S(1)} %psum.28), channel_id=1, replica_groups=mesh['leaf'=16,'sep'=8,'mode'=2] {'leaf'}, use_global_device_ids=true, to_apply=%region_8.9 | all-reduce | flops 256 | bytes 2048 | tf_op jit(solution)/shard_map/psum | solution.py:96
  266.5 29.4 %all_gather.7 = bf16[512,256]{1,0:T(8,128)(2,1)S(1)} all-gather(bf16[16,256]{1,0:T(8,128)(2,1)S(1)} %convolution_convert_fusion.4), channel_id=1, replica_groups=mesh['leaf'=16,'sep'=8,'mode'=2] {'leaf','mode'}, dimensions={0}, use_global_device_ids=true | all-gather | bytes 270336 | tf_op jit(solution)/shard_map/all_gather | solution.py:69
  295.9 85.1 %while.27 = (s32[]{:T(128)}, f32[512,256]{0,1:T(8,128)S(1)}, s32[16]{0:T(128)S(1)}, bf16[16,128,256]{2,1,0:T(8,128)(2,1)S(1)}, bf16[512,256]{1,0:T(8,128)(2,1)S(1)}, /*index=5*/s32[]{:T(128)}, s32[]{:T(128)}, s32[]{:T(128)}) while((s32[]{:T(128)}, f32[512,256]{0,1:T(8,128)S(1)}, s32[16]{0:T(128)S(1)}, bf16[16,128,256]{2,1,0:T(8,128)(2,1)S(1)}, ...), condition=%wide.region_10.11_spmd, body=%wide.region_9.10_spmd.sunk | while | flops 33652740 | bytes 2884751 | solution.py:65
  304.5 1.9 dynamic_update_slice.17
  309.8 1.9 dynamic_update_slice.17
  315.0 1.9 dynamic_update_slice.17
  330.8 2.2 dynamic_update_slice.17
  336.4 1.9 dynamic_update_slice.17
  346.9 1.9 dynamic_update_slice.17
  352.2 2.2 dynamic_update_slice.17
  357.8 1.9 dynamic_update_slice.17
  373.5 2.2 dynamic_update_slice.17
  382.3 82.8 %reduce-scatter.10.cloned.1.call-done = f32[16,256]{1,0:T(8,128)} async-done(((f32[512,256]{1,0:T(8,128)}), f32[16,256]{1,0:T(8,128)}) %reduce-scatter.10.cloned.1.call-update) | async-done | bytes 16400
  466.1 4.5 psum.30
  470.6 30.8 %psum.31 = f32[256]{0:T(256)S(1)} all-reduce(f32[256]{0:T(256)S(1)} %psum.30), channel_id=1, replica_groups=mesh['leaf'=16,'sep'=8,'mode'=2] {'leaf'}, use_global_device_ids=true, to_apply=%region_14.15 | all-reduce | flops 256 | bytes 2048 | tf_op jit(solution)/shard_map/psum | solution.py:96
  (181 shorter events, 90.8 us)
Async XLA Ops:
  7.2 140.5 %copy-start = (bf16[1,512,16]{1,2,0:T(8,128)(2,1)S(1)}, bf16[1,512,16]{1,2,0:T(8,128)(2,1)}, u32[]{:S(2)}) copy-start(bf16[1,512,16]{1,2,0:T(8,128)(2,1)} %param.17) | copy-start | bytes 49156
  7.2 6.3 %copy-start.4 = (s32[8,1]{0,1:T(1,128)S(1)}, s32[8,1]{0,1:T(1,128)}, u32[]{:S(2)}) copy-start(s32[8,1]{0,1:T(1,128)} %param.15) | copy-start | bytes 100
  7.2 6.5 %copy-start.5 = (s32[8]{0:T(128)S(1)}, s32[8]{0:T(128)}, u32[]{:S(2)}) copy-start(s32[8]{0:T(128)} %param.16) | copy-start | bytes 100
  7.2 16.3 %copy-start.2 = (f32[8,128]{1,0:T(8,128)S(1)}, f32[8,128]{1,0:T(8,128)}, u32[]{:S(2)}) copy-start(f32[8,128]{1,0:T(8,128)} %param.14) | copy-start | bytes 12292
  7.2 25.6 %reduce-scatter.6.cloned.1.call-start = ((), (), s32[]{:S(2)}) async-start(), calls=%async_computation.5 | async-start | bytes 3145728 | tf_op jit(solution)/shard_map/reduce_scatter | solution.py:13
  14.5 22.9 %all-to-all-start = ((s32[8,1,2]{2,1,0:T(1,128)}), s32[8,1,2]{2,1,0:T(1,128)S(1)}, u32[]{:S(2)}, u32[]{:S(2)}) async-start(s32[8,1,2]{2,1,0:T(1,128)} %bitcast.7), calls=%async_computation | async-start | bytes 8192 | tf_op jit(solution)/shard_map/all_to_all | solution.py:40
  34.5 9.6 %copy-start.1 = (bf16[1,16,256]{2,1,0:T(8,128)(2,1)S(1)}, bf16[1,16,256]{2,1,0:T(8,128)(2,1)}, u32[]{:S(2)}) copy-start(bf16[1,16,256]{2,1,0:T(8,128)(2,1)} %param.18) | copy-start | bytes 24580
  37.3 36.0 %all-to-all-start.1 = ((bf16[8,2,128,256]{3,1,2,0:T(2,128)(2,1)}), bf16[8,2,128,256]{3,1,2,0:T(2,128)(2,1)S(1)}, u32[]{:S(2)}, u32[]{:S(2)}) async-start(bf16[8,2,128,256]{3,1,2,0:T(2,128)(2,1)} %copy.30), calls=%async_computation.2 | async-start | bytes 2097152 | tf_op jit(solution)/shard_map/all_to_all | solution.py:37
  44.1 185.3 %reduce-scatter.8.cloned.1.call-start = ((), (), s32[]{:S(2)}) async-start(), calls=%async_computation.6 | async-start | bytes 540672 | tf_op jit(solution)/shard_map/reduce_scatter | solution.py:90
  73.6 192.1 %copy-start.3 = (bf16[1,2,256,256]{3,2,1,0:T(8,128)(2,1)S(1)}, bf16[1,2,256,256]{3,2,1,0:T(8,128)(2,1)}, u32[]{:S(2)}) copy-start(bf16[1,2,256,256]{3,2,1,0:T(8,128)(2,1)} %param.19) | copy-start | bytes 786436
  148.7 316.4 %reduce-scatter.10.cloned.1.call-start = ((), (), s32[]{:S(2)}) async-start(), calls=%async_computation.7 | async-start | bytes 540672
Sparse Core Ops, SparseCore 0:
  13.6 19.1 reduce-scatter.5
  148.9 80.5 reduce-scatter.7
  382.4 82.6 reduce-scatter.9
